TPU v7x, 32 devices: a whole 2x2x4 slice. The times are simulated.
32 devices in a mesh: leaf: 4 (over y, core), panel: 8 (over z, x).
Axes of the slice: x: 2, y: 2, z: 4, core: 2. Of those that a mesh axis runs over, the one named last changes fastest.
Arguments:
- root_entries: float32 [2048, 2048], P('leaf', 'panel'), as said below
- child_updates: bfloat16 [2048, 1024], P('leaf', 'panel'), as said below
- child_map: int32 [2, 1024], replicated, may hold values from 0 to 2047, as said below
- tile_pattern: int32 [2, 8, 8], replicated, may hold values 0 or 1
Outputs:
- factored: float32 [2048, 2048], P('leaf', 'panel')
Inputs may be any that keep to these rules, and one draw needn't show every extreme that they name: `root_entries`: symmetric and positive definite. `child_updates`: each child's block of 1024 rows is symmetric. `child_map`: each row holds 1024 distinct rows of the root front.
All inputs are finite; a program needn't handle non-finite values.
Results may differ from a plain program's by a relative error of at most 0.0003.
Values may be sent and summed in bfloat16 or wider, within the bound.
No kernel may reach another device: no remote copies, remote signals or barrier semaphores. Data moves between devices by JAX's collectives and lax.ppermute only.
A program may use at most 64 MiB of HBM per device.

v0:
```python
import jax
import jax.numpy as jnp
from jax import lax
from jax.sharding import PartitionSpec as P

PANEL = 256
STEPS = 5
HIGHEST = lax.Precision.HIGHEST


def spread_2(value, axis, root):
    mine = lax.axis_index(axis) == root
    return lax.psum(jnp.where(mine, value, jnp.zeros_like(value)), axis)


def select_columns(targets, column_ids):
    return (targets[:, None] == column_ids[None, :]).astype(jnp.bfloat16)


def pick_rows(piece, shifted, valid):
    row_count = piece.shape[0]
    picked = jnp.take(piece, jnp.clip(shifted, 0, row_count - 1), axis=0).astype(jnp.float32)
    return jnp.where(valid[:, None], picked, jnp.float32(0.0))


def make_solver(pivot_factor):

    def by_substitution(rows):
        return lax.linalg.triangular_solve(
            pivot_factor, rows, left_side=False, lower=True, transpose_a=True
        )

    return by_substitution


def finish_column(solved, pivot_factor, row_ids, last, offset, owns_pivot):
    column = jnp.where(row_ids[:, None] >= last, solved, jnp.float32(0.0))
    with_pivot = lax.dynamic_update_slice(column, pivot_factor, (offset, 0))
    return jnp.where(owns_pivot, with_pivot, column)


def per_device(root_entries, child_updates, child_map, tile_pattern):
    device_rows, panel_width = root_entries.shape
    child_cols = child_updates.shape[1]
    leaf_count = lax.axis_size("leaf")
    panel_count = lax.axis_size("panel")
    leaf_index = lax.axis_index("leaf")
    panel_index = lax.axis_index("panel")
    front_order = panel_width * panel_count
    child_order = child_cols * panel_count
    half_leaf = leaf_count // 2
    tile_width = child_order // tile_pattern.shape[1]
    own_child = leaf_index // half_leaf
    child_row = leaf_index % half_leaf * device_rows
    pattern = lax.dynamic_index_in_dim(tile_pattern, own_child, 0, keepdims=False)
    mirrored = jnp.maximum(pattern, pattern.T)
    tile_block = lax.dynamic_slice(
        mirrored,
        (child_row // tile_width, panel_index * (child_cols // tile_width)),
        (device_rows // tile_width, child_cols // tile_width),
    )
    spread = jnp.repeat(jnp.repeat(tile_block, tile_width, axis=0), tile_width, axis=1)
    kept_local = jnp.where(spread > 0, child_updates, jnp.zeros_like(child_updates))
    positions = jnp.full((2, front_order), -1, jnp.int32)
    counting = jnp.broadcast_to(jnp.arange(child_order, dtype=jnp.int32)[None, :], (2, child_order))
    positions = positions.at[jnp.arange(2)[:, None], child_map].set(counting)
    sources = lax.dynamic_slice_in_dim(positions, leaf_index * device_rows, device_rows, 1)
    row_ids = leaf_index * device_rows + jnp.arange(device_rows, dtype=jnp.int32)
    column_ids = panel_index * panel_width + jnp.arange(panel_width, dtype=jnp.int32)
    empty_block = jnp.zeros((device_rows, panel_width), jnp.float32)
    piece = lax.all_gather(kept_local, "leaf", axis=0, tiled=True)
    row_count = piece.shape[0]
    pieces = []
    for which in range(2):
        shifted = sources[which] + which * child_order
        valid = (sources[which] >= 0) & (shifted >= 0) & (shifted < row_count)
        shifted, valid = (shifted, valid)
        pieces.append(pick_rows(piece, shifted, valid))
    placed = jnp.stack(pieces).astype(jnp.bfloat16)
    total = empty_block
    piece = lax.all_gather(placed, "panel", axis=2, tiled=True)
    for which in range(2):
        targets = child_map[which]
        total = total + jnp.dot(
            piece[which], select_columns(targets, column_ids), preferred_element_type=jnp.float32
        )
    block = root_entries + total
    mirror_owner = panel_index * panel_width // device_rows
    mirror_offset = panel_index * panel_width % device_rows
    for step in range(STEPS):
        first = step * PANEL
        last = first + PANEL
        owner = first // device_rows
        offset = first % device_rows
        owns_pivot = leaf_index == owner
        diagonal = spread_2(block[offset : offset + PANEL], "leaf", owner)
        pivot_factor = jnp.linalg.cholesky(diagonal)
        apply_solve = make_solver(pivot_factor)
        column = finish_column(apply_solve(block), pivot_factor, row_ids, last, offset, owns_pivot)
        panel_rows = spread_2(column.astype(jnp.bfloat16), "panel", step).astype(column.dtype)
        mirror_rows = lax.dynamic_slice_in_dim(panel_rows, mirror_offset, panel_width, 0)
        mirror = spread_2(mirror_rows.astype(jnp.bfloat16), "leaf", mirror_owner).astype(
            mirror_rows.dtype
        )
        block = jnp.where(panel_index == step, column, block)
        update = jnp.dot(panel_rows, mirror.T, precision=HIGHEST)
        trailing = (row_ids[:, None] >= last) & (column_ids[None, :] >= last)
        block = jnp.where(trailing, block - update, block)
    done = STEPS * PANEL
    upper = (row_ids[:, None] < done) & (column_ids[None, :] >= done)
    return jnp.where(upper, jnp.float32(0.0), block)


def solution(mesh):
    placed = (P("leaf", "panel"), P("leaf", "panel"), P(), P())
    return jax.shard_map(
        per_device, mesh=mesh, in_specs=placed, out_specs=P("leaf", "panel"), check_vma=False
    )
```

profile of v0, /device:TPU:0, one launch (start us, length us, event | category | flops | bytes accessed | tf_op | source)
XLA Modules:
  0.0 1110.6 jit_solution(8116327354740606950)
XLA Ops:
  32.9 51.8 %all-gather.2.cloned.1.call-done = bf16[2,512,1024]{2,1,0:T(8,128)(2,1)} async-done(((bf16[2,512,128]{2,1,0:T(8,128)(2,1)}), bf16[2,512,1024]{2,1,0:T(8,128)(2,1)}) %all-gather.2.cloned.1.call-update) | async-done | bytes 2097168 | tf_op jit(solution)/shard_map/all_gather | solution.py:81
  88.8 29.7 %all-reduce.17.cloned.1.call-done = f32[256,256]{0,1:T(8,128)} async-done(((f32[256,256]{0,1:T(8,128)}), f32[256,256]{0,1:T(8,128)}) %all-reduce.17.cloned.1.call-update) | async-done | bytes 262160 | tf_op jit(solution)/shard_map/psum | solution.py:13
  120.6 11.7 %cholesky.256 = f32[128,128]{1,0:T(8,128)S(1)} custom-call(f32[128,128]{1,0:T(8,128)S(1)} %cholesky.422), custom_call_target="Cholesky" | custom-call | tf_op jit(solution)/shard_map/jit(cholesky)/cholesky | solution.py:97
  142.6 11.7 %cholesky.273 = f32[128,128]{1,0:T(8,128)S(1)} custom-call(f32[128,128]{1,0:T(8,128)S(1)} %convolution_subtract_fusion.14), custom_call_target="Cholesky" | custom-call | tf_op jit(solution)/shard_map/jit(cholesky)/cholesky | solution.py:97
  162.1 19.7 %custom-call.20 = f32[2,128,128]{1,2,0:T(8,128)S(1)} custom-call(f32[2,128,128]{2,1,0:T(8,128)S(1)} %get-tuple-element.40), custom_call_target="InvertDiagBlocksLowerTriangular" | custom-call | tf_op jit(solution)/shard_map/triangular_solve/custom-call.0 | solution.py:29
  184.0 70.6 %all-reduce.19.cloned.1.call-done = bf16[512,256]{0,1:T(8,128)(2,1)} async-done(((bf16[512,256]{0,1:T(8,128)(2,1)}), bf16[512,256]{0,1:T(8,128)(2,1)}) %all-reduce.19.cloned.1.call-update) | async-done | bytes 262160 | tf_op jit(solution)/shard_map/psum | solution.py:13
  256.3 31.2 %all-reduce.21.cloned.1.call-done = bf16[256,256]{0,1:T(8,128)(2,1)} async-done(((bf16[256,256]{0,1:T(8,128)(2,1)}), bf16[256,256]{0,1:T(8,128)(2,1)}) %all-reduce.21.cloned.1.call-update) | async-done | bytes 131088 | tf_op jit(solution)/shard_map/psum | solution.py:13
  289.6 32.2 %all-reduce.23.cloned.1.call-done = f32[256,256]{0,1:T(8,128)} async-done(((f32[256,256]{0,1:T(8,128)}), f32[256,256]{0,1:T(8,128)}) %all-reduce.23.cloned.1.call-update) | async-done | bytes 262160 | tf_op jit(solution)/shard_map/psum | solution.py:13
  323.9 11.7 %cholesky.290 = f32[128,128]{1,0:T(8,128)S(1)} custom-call(f32[128,128]{1,0:T(8,128)S(1)} %cholesky.425), custom_call_target="Cholesky" | custom-call | tf_op jit(solution)/shard_map/jit(cholesky)/cholesky | solution.py:97
  345.9 11.7 %cholesky.307 = f32[128,128]{1,0:T(8,128)S(1)} custom-call(f32[128,128]{1,0:T(8,128)S(1)} %convolution_subtract_fusion.13), custom_call_target="Cholesky" | custom-call | tf_op jit(solution)/shard_map/jit(cholesky)/cholesky | solution.py:97
  365.5 19.7 %custom-call.22 = f32[2,128,128]{1,2,0:T(8,128)S(1)} custom-call(f32[2,128,128]{2,1,0:T(8,128)S(1)} %get-tuple-element.41), custom_call_target="InvertDiagBlocksLowerTriangular" | custom-call | tf_op jit(solution)/shard_map/triangular_solve/custom-call.0 | solution.py:29
  387.4 70.7 %all-reduce.25.cloned.1.call-done = bf16[512,256]{0,1:T(8,128)(2,1)} async-done(((bf16[512,256]{0,1:T(8,128)(2,1)}), bf16[512,256]{0,1:T(8,128)(2,1)}) %all-reduce.25.cloned.1.call-update) | async-done | bytes 262160 | tf_op jit(solution)/shard_map/psum | solution.py:13
  459.8 31.5 %all-reduce.27.cloned.1.call-done = bf16[256,256]{0,1:T(8,128)(2,1)} async-done(((bf16[256,256]{0,1:T(8,128)(2,1)}), bf16[256,256]{0,1:T(8,128)(2,1)}) %all-reduce.27.cloned.1.call-update) | async-done | bytes 131088 | tf_op jit(solution)/shard_map/psum | solution.py:13
  493.3 32.3 %all-reduce.29.cloned.1.call-done = f32[256,256]{0,1:T(8,128)} async-done(((f32[256,256]{0,1:T(8,128)}), f32[256,256]{0,1:T(8,128)}) %all-reduce.29.cloned.1.call-update) | async-done | bytes 262160 | tf_op jit(solution)/shard_map/psum | solution.py:13
  527.7 11.7 %cholesky.324 = f32[128,128]{1,0:T(8,128)S(1)} custom-call(f32[128,128]{1,0:T(8,128)S(1)} %cholesky.428), custom_call_target="Cholesky" | custom-call | tf_op jit(solution)/shard_map/jit(cholesky)/cholesky | solution.py:97
  539.4 9.8 custom-call.23
  549.7 11.7 %cholesky.341 = f32[128,128]{1,0:T(8,128)S(1)} custom-call(f32[128,128]{1,0:T(8,128)S(1)} %convolution_subtract_fusion.12), custom_call_target="Cholesky" | custom-call | tf_op jit(solution)/shard_map/jit(cholesky)/cholesky | solution.py:97
  569.1 19.7 %custom-call.24 = f32[2,128,128]{1,2,0:T(8,128)S(1)} custom-call(f32[2,128,128]{2,1,0:T(8,128)S(1)} %get-tuple-element.42), custom_call_target="InvertDiagBlocksLowerTriangular" | custom-call | tf_op jit(solution)/shard_map/triangular_solve/custom-call.0 | solution.py:29
  591.0 70.6 %all-reduce.31.cloned.1.call-done = bf16[512,256]{0,1:T(8,128)(2,1)} async-done(((bf16[512,256]{0,1:T(8,128)(2,1)}), bf16[512,256]{0,1:T(8,128)(2,1)}) %all-reduce.31.cloned.1.call-update) | async-done | bytes 262160 | tf_op jit(solution)/shard_map/psum | solution.py:13
  663.3 31.2 %all-reduce.33.cloned.1.call-done = bf16[256,256]{0,1:T(8,128)(2,1)} async-done(((bf16[256,256]{0,1:T(8,128)(2,1)}), bf16[256,256]{0,1:T(8,128)(2,1)}) %all-reduce.33.cloned.1.call-update) | async-done | bytes 131088 | tf_op jit(solution)/shard_map/psum | solution.py:13
  696.6 32.4 %all-reduce.35.cloned.1.call-done = f32[256,256]{0,1:T(8,128)} async-done(((f32[256,256]{0,1:T(8,128)}), f32[256,256]{0,1:T(8,128)}) %all-reduce.35.cloned.1.call-update) | async-done | bytes 262160 | tf_op jit(solution)/shard_map/psum | solution.py:13
  731.0 11.7 %cholesky.358 = f32[128,128]{1,0:T(8,128)S(1)} custom-call(f32[128,128]{1,0:T(8,128)S(1)} %cholesky.431), custom_call_target="Cholesky" | custom-call | tf_op jit(solution)/shard_map/jit(cholesky)/cholesky | solution.py:97
  753.1 11.7 %cholesky.375 = f32[128,128]{1,0:T(8,128)S(1)} custom-call(f32[128,128]{1,0:T(8,128)S(1)} %convolution_subtract_fusion.11), custom_call_target="Cholesky" | custom-call | tf_op jit(solution)/shard_map/jit(cholesky)/cholesky | solution.py:97
  772.5 19.7 %custom-call.26 = f32[2,128,128]{1,2,0:T(8,128)S(1)} custom-call(f32[2,128,128]{2,1,0:T(8,128)S(1)} %get-tuple-element.43), custom_call_target="InvertDiagBlocksLowerTriangular" | custom-call | tf_op jit(solution)/shard_map/triangular_solve/custom-call.0 | solution.py:29
  794.4 70.7 %all-reduce.37.cloned.1.call-done = bf16[512,256]{0,1:T(8,128)(2,1)} async-done(((bf16[512,256]{0,1:T(8,128)(2,1)}), bf16[512,256]{0,1:T(8,128)(2,1)}) %all-reduce.37.cloned.1.call-update) | async-done | bytes 262160 | tf_op jit(solution)/shard_map/psum | solution.py:13
  866.7 31.5 %all-reduce.39.cloned.1.call-done = bf16[256,256]{0,1:T(8,128)(2,1)} async-done(((bf16[256,256]{0,1:T(8,128)(2,1)}), bf16[256,256]{0,1:T(8,128)(2,1)}) %all-reduce.39.cloned.1.call-update) | async-done | bytes 131088 | tf_op jit(solution)/shard_map/psum | solution.py:13
  900.3 32.1 %all-reduce.41.cloned.1.call-done = f32[256,256]{0,1:T(8,128)} async-done(((f32[256,256]{0,1:T(8,128)}), f32[256,256]{0,1:T(8,128)}) %all-reduce.41.cloned.1.call-update) | async-done | bytes 262160 | tf_op jit(solution)/shard_map/psum | solution.py:13
  934.5 11.7 %cholesky.392 = f32[128,128]{1,0:T(8,128)S(1)} custom-call(f32[128,128]{1,0:T(8,128)S(1)} %cholesky.434), custom_call_target="Cholesky" | custom-call | tf_op jit(solution)/shard_map/jit(cholesky)/cholesky | solution.py:97
  956.5 11.7 %cholesky.409 = f32[128,128]{1,0:T(8,128)S(1)} custom-call(f32[128,128]{1,0:T(8,128)S(1)} %convolution_subtract_fusion.10), custom_call_target="Cholesky" | custom-call | tf_op jit(solution)/shard_map/jit(cholesky)/cholesky | solution.py:97
  976.0 19.7 %custom-call.28 = f32[2,128,128]{1,2,0:T(8,128)S(1)} custom-call(f32[2,128,128]{2,1,0:T(8,128)S(1)} %get-tuple-element.44), custom_call_target="InvertDiagBlocksLowerTriangular" | custom-call | tf_op jit(solution)/shard_map/triangular_solve/custom-call.0 | solution.py:29
  997.9 70.6 %all-reduce.43.cloned.1.call-done = bf16[512,256]{0,1:T(8,128)(2,1)} async-done(((bf16[512,256]{0,1:T(8,128)(2,1)}), bf16[512,256]{0,1:T(8,128)(2,1)}) %all-reduce.43.cloned.1.call-update) | async-done | bytes 262160 | tf_op jit(solution)/shard_map/psum | solution.py:13
  1070.1 31.2 %all-reduce.45.cloned.1.call-done = bf16[256,256]{0,1:T(8,128)(2,1)} async-done(((bf16[256,256]{0,1:T(8,128)(2,1)}), bf16[256,256]{0,1:T(8,128)(2,1)}) %all-reduce.45.cloned.1.call-update) | async-done | bytes 131088 | tf_op jit(solution)/shard_map/psum | solution.py:13
  (274 shorter events, 164.8 us)
Async XLA Ops:
  6.5 78.1 %all-gather.2.cloned.1.call-start = ((), (), s32[]{:S(2)}) async-start(), calls=%async_computation | async-start | bytes 2359296 | tf_op jit(solution)/shard_map/all_gather | solution.py:81
  19.9 12.7 %copy-start.1 = (f32[512,256]{1,0:T(8,128)S(1)}, f32[512,256]{1,0:T(8,128)}, u32[]{:S(2)}) copy-start(f32[512,256]{1,0:T(8,128)} %param.9) | copy-start | bytes 1572868
  28.7 4.2 copy-start.2
  32.5 85.9 %all-reduce.17.cloned.1.call-start = ((), (), s32[]{:S(2)}) async-start(), calls=%async_computation.1 | async-start | bytes 524288 | tf_op jit(solution)/shard_map/psum | solution.py:13
  84.6 2.1 copy-start
  88.2 166.4 %all-reduce.19.cloned.1.call-start = ((), (), s32[]{:S(2)}) async-start(), calls=%async_computation.2 | async-start | bytes 524288 | tf_op jit(solution)/shard_map/psum | solution.py:13
  183.9 103.6 %all-reduce.21.cloned.1.call-start = ((), (), s32[]{:S(2)}) async-start(), calls=%async_computation.3 | async-start | bytes 262144 | tf_op jit(solution)/shard_map/psum | solution.py:13
  256.2 65.5 %all-reduce.23.cloned.1.call-start = ((), (), s32[]{:S(2)}) async-start(), calls=%async_computation.4 | async-start | bytes 524288 | tf_op jit(solution)/shard_map/psum | solution.py:13
  289.5 168.6 %all-reduce.25.cloned.1.call-start = ((), (), s32[]{:S(2)}) async-start(), calls=%async_computation.5 | async-start | bytes 524288 | tf_op jit(solution)/shard_map/psum | solution.py:13
  387.4 103.9 %all-reduce.27.cloned.1.call-start = ((), (), s32[]{:S(2)}) async-start(), calls=%async_computation.6 | async-start | bytes 262144 | tf_op jit(solution)/shard_map/psum | solution.py:13
  459.7 65.9 %all-reduce.29.cloned.1.call-start = ((), (), s32[]{:S(2)}) async-start(), calls=%async_computation.7 | async-start | bytes 524288 | tf_op jit(solution)/shard_map/psum | solution.py:13
  493.3 168.4 %all-reduce.31.cloned.1.call-start = ((), (), s32[]{:S(2)}) async-start(), calls=%async_computation.8 | async-start | bytes 524288 | tf_op jit(solution)/shard_map/psum | solution.py:13
  590.9 103.5 %all-reduce.33.cloned.1.call-start = ((), (), s32[]{:S(2)}) async-start(), calls=%async_computation.9 | async-start | bytes 262144 | tf_op jit(solution)/shard_map/psum | solution.py:13
  663.2 65.7 %all-reduce.35.cloned.1.call-start = ((), (), s32[]{:S(2)}) async-start(), calls=%async_computation.10 | async-start | bytes 524288 | tf_op jit(solution)/shard_map/psum | solution.py:13
  696.5 168.6 %all-reduce.37.cloned.1.call-start = ((), (), s32[]{:S(2)}) async-start(), calls=%async_computation.11 | async-start | bytes 524288 | tf_op jit(solution)/shard_map/psum | solution.py:13
  794.3 103.9 %all-reduce.39.cloned.1.call-start = ((), (), s32[]{:S(2)}) async-start(), calls=%async_computation.12 | async-start | bytes 262144 | tf_op jit(solution)/shard_map/psum | solution.py:13
  866.7 65.7 %all-reduce.41.cloned.1.call-start = ((), (), s32[]{:S(2)}) async-start(), calls=%async_computation.13 | async-start | bytes 524288 | tf_op jit(solution)/shard_map/psum | solution.py:13
  900.2 168.3 %all-reduce.43.cloned.1.call-start = ((), (), s32[]{:S(2)}) async-start(), calls=%async_computation.14 | async-start | bytes 524288 | tf_op jit(solution)/shard_map/psum | solution.py:13
  997.8 103.5 %all-reduce.45.cloned.1.call-start = ((), (), s32[]{:S(2)}) async-start(), calls=%async_computation.15 | async-start | bytes 262144 | tf_op jit(solution)/shard_map/psum | solution.py:13
Sparse Core Ops, SparseCore 0:
  32.7 51.9 all-gather.1
  88.3 30.1 all-reduce.16
  184.0 70.5 all-reduce.18
  256.8 30.6 all-reduce.20
  289.8 31.9 all-reduce.22
  387.5 70.5 all-reduce.24
  460.5 30.6 all-reduce.26
  493.6 31.9 all-reduce.28
  591.1 70.5 all-reduce.30
  663.8 30.6 all-reduce.32
  696.9 31.9 all-reduce.34
  794.4 70.5 all-reduce.36
  867.5 30.6 all-reduce.38
  900.4 31.9 all-reduce.40
  997.9 70.4 all-reduce.42
  1070.6 30.6 all-reduce.44
where the time goes:
time: 1120 us; the launch traced here: 1110 us
  waiting for transfers between devices  720 us (64%)
  other arithmetic  298 us (27%)
  local copies, waits for them, and re-layouts  41.2 us (4%)
  between operations  21.6 us (2%)
  matrix products  17.7 us (2%)
    psum x15, waiting for transfers between devices, spread_2(): return lax.psum(jnp.where(mine, value, jnp.zeros_like(value)), axis)  668 us
    another operation x35, other arithmetic, per_device(): pivot_factor = jnp.linalg.cholesky(diagonal)  173 us
    another operation x11, other arithmetic, by_substitution(): lax.linalg.triangular_solve(pivot_factor, rows, left_side=False, lower=Tr...  98.5 us
    all_gather x1, waiting for transfers between devices, per_device(): piece = lax.all_gather(placed, 'panel', axis=2, tiled=True)  51.8 us
  transfers between devices with their start and end apart: 16, of which 16 were waited for; matrix products, arithmetic and copies ran while one was open for 0% of the time, Pallas kernels for 0%

commit v1 on v0

--- a/solution.py
+++ b/solution.py
@@ -10,7 +10,7 @@
 
 def spread_2(value, axis, root):
     mine = lax.axis_index(axis) == root
-    return lax.psum(jnp.where(mine, value, jnp.zeros_like(value)), axis)
+    return jnp.sum(lax.all_gather(jnp.where(mine, value, jnp.zeros_like(value)), axis), axis=0)
 
 
 def select_columns(targets, column_ids):

time: 1120 us -> 794 us (0.71)
  waiting for transfers between devices: 720 us -> 373 us
  blocking collectives: 8.78 us -> 44.4 us
    psum x15 -> x0, waiting for transfers between devices: 668 us -> none  [spread_2(): return lax.psum(jnp.where(mine, value, jnp.zeros_like(value)), axis)]
    all_gather x0 -> x10, waiting for transfers between devices: none -> 321 us  [spread_2(): lax.all_gather(jnp.where(mine, value, jnp.zeros_like(value)), axis)]
    all_gather x0 -> x5, blocking collectives: none -> 35.8 us  [spread_2(): lax.all_gather(jnp.where(mine, value, jnp.zeros_like(value)), axis)]
    reduce_sum x0 -> x15, other arithmetic: none -> 16.8 us  [spread_2(): jnp.sum(lax.all_gather(jnp.where(mine, value, jnp.zeros_like(value)), axi...]
  transfers between devices with their start and end apart: 16 -> 11, of which waited for: 16 -> 11; matrix products, arithmetic and copies ran while one was open for 0% -> 0% of each run, Pallas kernels for 0% -> 0%
where the time goes in v1:
time: 794 us; the launch traced here: 790 us
  waiting for transfers between devices  373 us (47%)
  other arithmetic  303 us (38%)
  blocking collectives  44.4 us (6%)
  local copies, waits for them, and re-layouts  32.3 us (4%)
  between operations  20.9 us (3%)
  matrix products  13.9 us (2%)
    all_gather x10, waiting for transfers between devices, spread_2(): lax.all_gather(jnp.where(mine, value, jnp.zeros_like(value)), axis)  321 us
    another operation x35, other arithmetic, per_device(): pivot_factor = jnp.linalg.cholesky(diagonal)  173 us
    another operation x11, other arithmetic, by_substitution(): lax.linalg.triangular_solve(pivot_factor, rows, left_side=False, lower=Tr...  98.5 us
    all_gather x1, waiting for transfers between devices, per_device(): piece = lax.all_gather(placed, 'panel', axis=2, tiled=True)  52 us
    all_gather x5, blocking collectives, spread_2(): lax.all_gather(jnp.where(mine, value, jnp.zeros_like(value)), axis)  35.8 us
    another operation x41, local copies, waits for them, and re-layouts, by_substitution(): lax.linalg.triangular_solve(pivot_factor, rows, left_side=False, lower=Tr...  19.9 us
    reduce_sum x15, other arithmetic, spread_2(): jnp.sum(lax.all_gather(jnp.where(mine, value, jnp.zeros_like(value)), axi...  16.8 us
  transfers between devices with their start and end apart: 11, of which 11 were waited for; matrix products, arithmetic and copies ran while one was open for 0% of the time, Pallas kernels for 0%

profile of v1, /device:TPU:0, one launch (start us, length us, event | category | flops | bytes accessed | tf_op | source)
XLA Modules:
  0.0 789.7 jit_solution(14441636804188555690)
XLA Ops:
  19.9 8.6 %all_gather.96 = bf16[2048,128]{1,0:T(8,128)(2,1)S(1)} all-gather(bf16[512,128]{1,0:T(8,128)(2,1)S(1)} %broadcast_select_fusion), channel_id=1, replica_groups=mesh['leaf'=4,'panel'=8] {'leaf'}, dimensions={0}, use_global_device_ids=true | all-gather | bytes 655360 | tf_op jit(solution)/shard_map/all_gather | solution.py:71
  32.5 52.0 %all-gather.27.cloned.1.call-done = bf16[2,512,1024]{2,1,0:T(8,128)(2,1)} async-done(((bf16[2,512,128]{2,1,0:T(8,128)(2,1)}), bf16[2,512,1024]{2,1,0:T(8,128)(2,1)}) %all-gather.27.cloned.1.call-update) | async-done | bytes 2097168 | tf_op jit(solution)/shard_map/all_gather | solution.py:81
  88.4 14.5 %all-gather.29.cloned.1.call-done = f32[1024,256]{1,0:T(8,128)} async-done(((f32[256,256]{1,0:T(8,128)}), f32[1024,256]{1,0:T(8,128)}) %all-gather.29.cloned.1.call-update) | async-done | bytes 1048592 | tf_op jit(solution)/shard_map/all_gather | solution.py:13
  104.4 11.7 %cholesky.256 = f32[128,128]{1,0:T(8,128)S(1)} custom-call(f32[128,128]{1,0:T(8,128)S(1)} %cholesky.422), custom_call_target="Cholesky" | custom-call | tf_op jit(solution)/shard_map/jit(cholesky)/cholesky | solution.py:97
  116.1 9.8 %custom-call.19 = f32[1,128,128]{1,2,0:T(8,128)S(1)} custom-call(f32[1,128,128]{2,1,0:T(8,128)S(1)} %get-tuple-element.116), custom_call_target="InvertDiagBlocksLowerTriangular" | custom-call | tf_op jit(solution)/shard_map/jit(cholesky)/cholesky | solution.py:97
  126.4 11.7 %cholesky.273 = f32[128,128]{1,0:T(8,128)S(1)} custom-call(f32[128,128]{1,0:T(8,128)S(1)} %convolution_subtract_fusion.14), custom_call_target="Cholesky" | custom-call | tf_op jit(solution)/shard_map/jit(cholesky)/cholesky | solution.py:97
  144.8 19.7 %custom-call.20 = f32[2,128,128]{1,2,0:T(8,128)S(1)} custom-call(f32[2,128,128]{2,1,0:T(8,128)S(1)} %get-tuple-element.40), custom_call_target="InvertDiagBlocksLowerTriangular" | custom-call | tf_op jit(solution)/shard_map/triangular_solve/custom-call.0 | solution.py:29
  167.1 49.4 %all-gather.31.cloned.1.call-done = bf16[4096,256]{1,0:T(8,128)(2,1)} async-done(((bf16[512,256]{1,0:T(8,128)(2,1)}), bf16[4096,256]{1,0:T(8,128)(2,1)}) %all-gather.31.cloned.1.call-update) | async-done | bytes 2097168 | tf_op jit(solution)/shard_map/all_gather | solution.py:13
  226.8 14.9 %all-gather.33.cloned.1.call-done = f32[1024,256]{1,0:T(8,128)} async-done(((f32[256,256]{1,0:T(8,128)}), f32[1024,256]{1,0:T(8,128)}) %all-gather.33.cloned.1.call-update) | async-done | bytes 1048592 | tf_op jit(solution)/shard_map/all_gather | solution.py:13
  243.2 11.7 %cholesky.290 = f32[128,128]{1,0:T(8,128)S(1)} custom-call(f32[128,128]{1,0:T(8,128)S(1)} %cholesky.425), custom_call_target="Cholesky" | custom-call | tf_op jit(solution)/shard_map/jit(cholesky)/cholesky | solution.py:97
  255.0 9.8 %custom-call.21 = f32[1,128,128]{1,2,0:T(8,128)S(1)} custom-call(f32[1,128,128]{2,1,0:T(8,128)S(1)} %get-tuple-element.112), custom_call_target="InvertDiagBlocksLowerTriangular" | custom-call | tf_op jit(solution)/shard_map/jit(cholesky)/cholesky | solution.py:97
  265.3 11.7 %cholesky.307 = f32[128,128]{1,0:T(8,128)S(1)} custom-call(f32[128,128]{1,0:T(8,128)S(1)} %convolution_subtract_fusion.13), custom_call_target="Cholesky" | custom-call | tf_op jit(solution)/shard_map/jit(cholesky)/cholesky | solution.py:97
  283.8 19.7 %custom-call.22 = f32[2,128,128]{1,2,0:T(8,128)S(1)} custom-call(f32[2,128,128]{2,1,0:T(8,128)S(1)} %get-tuple-element.41), custom_call_target="InvertDiagBlocksLowerTriangular" | custom-call | tf_op jit(solution)/shard_map/triangular_solve/custom-call.0 | solution.py:29
  306.0 49.4 %all-gather.35.cloned.1.call-done = bf16[4096,256]{1,0:T(8,128)(2,1)} async-done(((bf16[512,256]{1,0:T(8,128)(2,1)}), bf16[4096,256]{1,0:T(8,128)(2,1)}) %all-gather.35.cloned.1.call-update) | async-done | bytes 2097168 | tf_op jit(solution)/shard_map/all_gather | solution.py:13
  365.8 14.9 %all-gather.37.cloned.1.call-done = f32[1024,256]{1,0:T(8,128)} async-done(((f32[256,256]{1,0:T(8,128)}), f32[1024,256]{1,0:T(8,128)}) %all-gather.37.cloned.1.call-update) | async-done | bytes 1048592 | tf_op jit(solution)/shard_map/all_gather | solution.py:13
  382.2 11.7 %cholesky.324 = f32[128,128]{1,0:T(8,128)S(1)} custom-call(f32[128,128]{1,0:T(8,128)S(1)} %cholesky.428), custom_call_target="Cholesky" | custom-call | tf_op jit(solution)/shard_map/jit(cholesky)/cholesky | solution.py:97
  393.9 9.8 %custom-call.23 = f32[1,128,128]{1,2,0:T(8,128)S(1)} custom-call(f32[1,128,128]{2,1,0:T(8,128)S(1)} %get-tuple-element.108), custom_call_target="InvertDiagBlocksLowerTriangular" | custom-call | tf_op jit(solution)/shard_map/jit(cholesky)/cholesky | solution.py:97
  404.2 11.7 %cholesky.341 = f32[128,128]{1,0:T(8,128)S(1)} custom-call(f32[128,128]{1,0:T(8,128)S(1)} %convolution_subtract_fusion.12), custom_call_target="Cholesky" | custom-call | tf_op jit(solution)/shard_map/jit(cholesky)/cholesky | solution.py:97
  422.5 19.7 %custom-call.24 = f32[2,128,128]{1,2,0:T(8,128)S(1)} custom-call(f32[2,128,128]{2,1,0:T(8,128)S(1)} %get-tuple-element.42), custom_call_target="InvertDiagBlocksLowerTriangular" | custom-call | tf_op jit(solution)/shard_map/triangular_solve/custom-call.0 | solution.py:29
  444.8 49.4 %all-gather.39.cloned.1.call-done = bf16[4096,256]{1,0:T(8,128)(2,1)} async-done(((bf16[512,256]{1,0:T(8,128)(2,1)}), bf16[4096,256]{1,0:T(8,128)(2,1)}) %all-gather.39.cloned.1.call-update) | async-done | bytes 2097168 | tf_op jit(solution)/shard_map/all_gather | solution.py:13
  504.5 14.9 %all-gather.41.cloned.1.call-done = f32[1024,256]{1,0:T(8,128)} async-done(((f32[256,256]{1,0:T(8,128)}), f32[1024,256]{1,0:T(8,128)}) %all-gather.41.cloned.1.call-update) | async-done | bytes 1048592 | tf_op jit(solution)/shard_map/all_gather | solution.py:13
  520.9 11.7 %cholesky.358 = f32[128,128]{1,0:T(8,128)S(1)} custom-call(f32[128,128]{1,0:T(8,128)S(1)} %cholesky.431), custom_call_target="Cholesky" | custom-call | tf_op jit(solution)/shard_map/jit(cholesky)/cholesky | solution.py:97
  532.7 9.8 %custom-call.25 = f32[1,128,128]{1,2,0:T(8,128)S(1)} custom-call(f32[1,128,128]{2,1,0:T(8,128)S(1)} %get-tuple-element.104), custom_call_target="InvertDiagBlocksLowerTriangular" | custom-call | tf_op jit(solution)/shard_map/jit(cholesky)/cholesky | solution.py:97
  543.0 11.7 %cholesky.375 = f32[128,128]{1,0:T(8,128)S(1)} custom-call(f32[128,128]{1,0:T(8,128)S(1)} %convolution_subtract_fusion.11), custom_call_target="Cholesky" | custom-call | tf_op jit(solution)/shard_map/jit(cholesky)/cholesky | solution.py:97
  561.3 19.7 %custom-call.26 = f32[2,128,128]{1,2,0:T(8,128)S(1)} custom-call(f32[2,128,128]{2,1,0:T(8,128)S(1)} %get-tuple-element.43), custom_call_target="InvertDiagBlocksLowerTriangular" | custom-call | tf_op jit(solution)/shard_map/triangular_solve/custom-call.0 | solution.py:29
  583.6 49.4 %all-gather.43.cloned.1.call-done = bf16[4096,256]{1,0:T(8,128)(2,1)} async-done(((bf16[512,256]{1,0:T(8,128)(2,1)}), bf16[4096,256]{1,0:T(8,128)(2,1)}) %all-gather.43.cloned.1.call-update) | async-done | bytes 2097168 | tf_op jit(solution)/shard_map/all_gather | solution.py:13
  643.3 14.9 %all-gather.45.cloned.1.call-done = f32[1024,256]{1,0:T(8,128)} async-done(((f32[256,256]{1,0:T(8,128)}), f32[1024,256]{1,0:T(8,128)}) %all-gather.45.cloned.1.call-update) | async-done | bytes 1048592 | tf_op jit(solution)/shard_map/all_gather | solution.py:13
  659.7 11.7 %cholesky.392 = f32[128,128]{1,0:T(8,128)S(1)} custom-call(f32[128,128]{1,0:T(8,128)S(1)} %cholesky.434), custom_call_target="Cholesky" | custom-call | tf_op jit(solution)/shard_map/jit(cholesky)/cholesky | solution.py:97
  671.5 9.8 %custom-call.27 = f32[1,128,128]{1,2,0:T(8,128)S(1)} custom-call(f32[1,128,128]{2,1,0:T(8,128)S(1)} %get-tuple-element.100), custom_call_target="InvertDiagBlocksLowerTriangular" | custom-call | tf_op jit(solution)/shard_map/jit(cholesky)/cholesky | solution.py:97
  681.8 11.7 %cholesky.409 = f32[128,128]{1,0:T(8,128)S(1)} custom-call(f32[128,128]{1,0:T(8,128)S(1)} %convolution_subtract_fusion.10), custom_call_target="Cholesky" | custom-call | tf_op jit(solution)/shard_map/jit(cholesky)/cholesky | solution.py:97
  700.7 19.7 %custom-call.28 = f32[2,128,128]{1,2,0:T(8,128)S(1)} custom-call(f32[2,128,128]{2,1,0:T(8,128)S(1)} %get-tuple-element.44), custom_call_target="InvertDiagBlocksLowerTriangular" | custom-call | tf_op jit(solution)/shard_map/triangular_solve/custom-call.0 | solution.py:29
  722.9 49.4 %all-gather.47.cloned.1.call-done = bf16[4096,256]{1,0:T(8,128)(2,1)} async-done(((bf16[512,256]{1,0:T(8,128)(2,1)}), bf16[4096,256]{1,0:T(8,128)(2,1)}) %all-gather.47.cloned.1.call-update) | async-done | bytes 2097168 | tf_op jit(solution)/shard_map/all_gather | solution.py:13
  (237 shorter events, 141.8 us)
Async XLA Ops:
  6.5 78.0 %all-gather.27.cloned.1.call-start = ((), (), s32[]{:S(2)}) async-start(), calls=%async_computation | async-start | bytes 2359296 | tf_op jit(solution)/shard_map/all_gather | solution.py:81
  19.9 12.6 %copy-start.2 = (s32[2,1024]{1,0:T(2,128)S(1)}, s32[2,1024]{1,0:T(2,128)}, u32[]{:S(2)}) copy-start(s32[2,1024]{1,0:T(2,128)} %param.11) | copy-start | bytes 24580
  31.2 55.2 %copy-start = (f32[512,256]{1,0:T(8,128)S(1)}, f32[512,256]{1,0:T(8,128)}, u32[]{:S(2)}) copy-start(f32[512,256]{1,0:T(8,128)} %param.9) | copy-start | bytes 1572868
  32.4 70.4 %all-gather.29.cloned.1.call-start = ((), (), s32[]{:S(2)}) async-start(), calls=%async_computation.1 | async-start | bytes 1310720 | tf_op jit(solution)/shard_map/all_gather | solution.py:13
  84.5 1.9 copy-start.1
  87.8 128.7 %all-gather.31.cloned.1.call-start = ((), (), s32[]{:S(2)}) async-start(), calls=%async_computation.2 | async-start | bytes 2359296 | tf_op jit(solution)/shard_map/all_gather | solution.py:13
  167.0 74.7 %all-gather.33.cloned.1.call-start = ((), (), s32[]{:S(2)}) async-start(), calls=%async_computation.3 | async-start | bytes 1310720 | tf_op jit(solution)/shard_map/all_gather | solution.py:13
  226.7 128.7 %all-gather.35.cloned.1.call-start = ((), (), s32[]{:S(2)}) async-start(), calls=%async_computation.4 | async-start | bytes 2359296 | tf_op jit(solution)/shard_map/all_gather | solution.py:13
  306.0 74.7 %all-gather.37.cloned.1.call-start = ((), (), s32[]{:S(2)}) async-start(), calls=%async_computation.5 | async-start | bytes 1310720 | tf_op jit(solution)/shard_map/all_gather | solution.py:13
  365.7 128.5 %all-gather.39.cloned.1.call-start = ((), (), s32[]{:S(2)}) async-start(), calls=%async_computation.6 | async-start | bytes 2359296 | tf_op jit(solution)/shard_map/all_gather | solution.py:13
  444.7 74.7 %all-gather.41.cloned.1.call-start = ((), (), s32[]{:S(2)}) async-start(), calls=%async_computation.7 | async-start | bytes 1310720 | tf_op jit(solution)/shard_map/all_gather | solution.py:13
  504.5 128.5 %all-gather.43.cloned.1.call-start = ((), (), s32[]{:S(2)}) async-start(), calls=%async_computation.8 | async-start | bytes 2359296 | tf_op jit(solution)/shard_map/all_gather | solution.py:13
  583.5 74.7 %all-gather.45.cloned.1.call-start = ((), (), s32[]{:S(2)}) async-start(), calls=%async_computation.9 | async-start | bytes 1310720 | tf_op jit(solution)/shard_map/all_gather | solution.py:13
  643.2 129.1 %all-gather.47.cloned.1.call-start = ((), (), s32[]{:S(2)}) async-start(), calls=%async_computation.10 | async-start | bytes 2359296 | tf_op jit(solution)/shard_map/all_gather | solution.py:13
Sparse Core Ops, SparseCore 0:
  32.5 51.9 all-gather.26
  87.9 14.9 all-gather.28
  167.1 49.2 all-gather.30
  226.8 14.7 all-gather.32
  306.1 49.2 all-gather.34
  365.8 14.7 all-gather.36
  444.8 49.2 all-gather.38
  504.6 14.7 all-gather.40
  583.7 49.2 all-gather.42
  643.4 14.7 all-gather.44
  723.0 49.2 all-gather.46
